TPU v7x, 512 devices: a whole 4x8x8 slice. The times are simulated.
512 devices in a mesh: prow: 32 (over y, x), pcol: 16 (over z, core).
Axes of the slice: x: 4, y: 8, z: 8, core: 2. Of those that a mesh axis runs over, the one named last changes fastest.
Arguments:
- matrix: bfloat16 [4, 8192, 4, 4096], P(None, 'prow', None, 'pcol'), may hold values from -6 to 6
- pivots: int32 [2, 256], replicated, may hold values from 0 to 32767, as said below
- lower_inverse: bfloat16 [2, 256, 256], replicated, as said below
- upper_inverse: bfloat16 [2, 256, 256], replicated, as said below
Outputs:
- factored: bfloat16 [4, 8192, 4, 4096], P(None, 'prow', None, 'pcol')
Inputs may be any that keep to these rules, and one draw needn't show every extreme that they name: For each panel k and each i, pivots[k, i] is either k * 256 + i or a row at or after (k + 1) * 256; entry 0 of each list is k * 256; the rows of one panel's list are distinct, and each list names row 32767. Each lower_inverse[k] is unit lower triangular. Each upper_inverse[k] is upper triangular with positive diagonal.
All inputs are finite; a program needn't handle non-finite values.
Results may differ from a plain program's by a relative error of at most 0.0079.
Values may be sent and summed in bfloat16 or wider, within the bound.
A program may use at most 64 MiB of HBM per device.

v0:
```python
import jax
import jax.numpy as jnp
from jax import lax
from jax.sharding import PartitionSpec as P


def spread(block, axis, source):
    block = jnp.where(lax.axis_index(axis) == source, block, jnp.zeros_like(block))
    return lax.psum(block, axis)


def local(matrix, pivots, lower_inverse, upper_inverse):
    row_count = lax.axis_size("prow")
    col_count = lax.axis_size("pcol")
    my_row = lax.axis_index("prow")
    my_col = lax.axis_index("pcol")
    blocks_down, block, blocks_across, _ = matrix.shape
    local_rows = blocks_down * block
    local_cols = blocks_across * block
    current = matrix.reshape(local_rows, local_cols)
    row_place = jnp.arange(local_rows)
    col_place = jnp.arange(local_cols)
    global_rows = (row_place // block * row_count + my_row) * block + row_place % block
    global_cols = (col_place // block * col_count + my_col) * block + col_place % block
    for panel in range(pivots.shape[0]):
        start = panel * block
        chosen = pivots[panel]
        block_row = chosen // block
        is_mine = block_row % row_count == my_row
        local_index = block_row // row_count * block + chosen % block
        safe_index = jnp.where(is_mine, local_index, 0)
        picked = jnp.where(is_mine[:, None], current[safe_index], jnp.zeros((), jnp.bfloat16))
        top_holder = panel % row_count
        top_first = panel // row_count * block
        is_top = my_row == top_holder
        top_local = current[top_first : top_first + block]
        incoming = lax.psum(picked, "prow").astype(jnp.float32)
        old_top = spread(top_local, "prow", top_holder)
        incoming = incoming.astype(jnp.bfloat16)
        target = jnp.where(is_mine, local_index, local_rows)
        current = current.at[target].set(old_top, mode="drop")
        top_now = current[top_first : top_first + block]
        current = current.at[top_first : top_first + block].set(
            jnp.where(is_top, incoming, top_now)
        )
        panel_holder = panel % col_count
        panel_first = panel // col_count * block
        panel_cols = current[:, panel_first : panel_first + block]
        factor = jnp.dot(
            panel_cols, upper_inverse[panel], preferred_element_type=jnp.float32
        ).astype(jnp.bfloat16)
        lower = spread(factor, "pcol", panel_holder)
        top_rows_now = current[top_first : top_first + block]
        upper_local = jnp.dot(
            lower_inverse[panel], top_rows_now, preferred_element_type=jnp.float32
        ).astype(jnp.bfloat16)
        upper = spread(upper_local, "prow", top_holder)
        row_mask = global_rows >= start + block
        col_mask = global_cols >= start + block
        product = jnp.dot(lower, upper, preferred_element_type=jnp.float32)
        changed = (current.astype(jnp.float32) - product).astype(jnp.bfloat16)
        current = jnp.where(row_mask[:, None] & col_mask[None, :], changed, current)
        panel_now = current[:, panel_first : panel_first + block]
        is_panel = my_col == panel_holder
        current = current.at[:, panel_first : panel_first + block].set(
            jnp.where(is_panel & row_mask[:, None], lower, panel_now)
        )
        top_now = current[top_first : top_first + block]
        current = current.at[top_first : top_first + block].set(
            jnp.where(is_top & col_mask[None, :], upper, top_now)
        )
    return current.reshape(matrix.shape)


def solution(mesh):
    in_specs = (P(None, "prow", None, "pcol"), P(), P(), P())
    out_specs = P(None, "prow", None, "pcol")
    return jax.shard_map(local, mesh=mesh, in_specs=in_specs, out_specs=out_specs, check_vma=False)
```

profile of v0, /device:TPU:64, one launch (start us, length us, event | category | flops | bytes accessed | tf_op | source)
XLA Modules:
  0.0 935.4 jit_solution(9245979962297047601)
XLA Ops:
  8.1 2.1 copy.23
  10.2 1.3 slice_select_fusion.4
  12.4 1.2 gather_fusion
  14.6 164.6 %all-reduce.19.cloned.1.call-done = (bf16[256,1024]{1,0:T(8,128)(2,1)}, bf16[256,1024]{1,0:T(8,128)(2,1)}) async-done(((bf16[256,1024]{1,0:T(8,128)(2,1)}, bf16[256,1024]{1,0:T(8,128)(2,1)}), (bf16[256,1024]{1,0:T(8,128)(2,1)}, bf16[256,1024]{1,0:T(8,128)(2,1)})) %all-reduce.19.cloned.1.call-update) | async-done | bytes 1048592 | tf_op jit(solution)/shard_map/psum | solution.py:9
  179.2 3.3 scatter_fusion
  182.6 1.1 fusion.3
  183.9 1.1 fusion
  185.9 109.8 %all-reduce.9.cloned.1.call-done = bf16[1024,256]{1,0:T(8,128)(2,1)} async-done(((bf16[1024,256]{1,0:T(8,128)(2,1)}), bf16[1024,256]{1,0:T(8,128)(2,1)}) %all-reduce.9.cloned.1.call-update) | async-done | bytes 524304 | tf_op jit(solution)/shard_map/psum | solution.py:9
  295.8 164.5 %all-reduce.11.cloned.1.call-done = bf16[256,1024]{1,0:T(8,128)(2,1)} async-done(((bf16[256,1024]{1,0:T(8,128)(2,1)}), bf16[256,1024]{1,0:T(8,128)(2,1)}) %all-reduce.11.cloned.1.call-update) | async-done | bytes 524304 | tf_op jit(solution)/shard_map/psum | solution.py:9
  460.3 3.6 and_select_fusion
  463.8 2.9 fusion.6
  466.8 2.3 broadcast_select_fusion.2
  469.1 3.4 gather_fusion.1
  473.5 158.0 %all-reduce.17.cloned.1.call-done = (bf16[256,1024]{1,0:T(8,128)(2,1)}, bf16[256,1024]{1,0:T(8,128)(2,1)}) async-done(((bf16[256,1024]{1,0:T(8,128)(2,1)}, bf16[256,1024]{1,0:T(8,128)(2,1)}), (bf16[256,1024]{1,0:T(8,128)(2,1)}, bf16[256,1024]{1,0:T(8,128)(2,1)})) %all-reduce.17.cloned.1.call-update) | async-done | bytes 1048592 | tf_op jit(solution)/shard_map/psum | solution.py:9
  631.5 5.4 scatter_fusion.1
  636.9 2.2 fusion.5
  639.1 2.0 fusion.11
  641.1 2.2 fusion.1
  644.0 110.1 %all-reduce.13.cloned.1.call-done = bf16[1024,256]{0,1:T(8,128)(2,1)} async-done(((bf16[1024,256]{0,1:T(8,128)(2,1)}), bf16[1024,256]{0,1:T(8,128)(2,1)}) %all-reduce.13.cloned.1.call-update) | async-done | bytes 524304 | tf_op jit(solution)/shard_map/psum | solution.py:9
  754.1 164.3 %all-reduce.15.cloned.1.call-done = bf16[256,1024]{1,0:T(8,128)(2,1)} async-done(((bf16[256,1024]{1,0:T(8,128)(2,1)}), bf16[256,1024]{1,0:T(8,128)(2,1)}) %all-reduce.15.cloned.1.call-update) | async-done | bytes 524304 | tf_op jit(solution)/shard_map/psum | solution.py:9
  918.5 3.7 and_select_fusion.1
  922.5 1.8 select_select_fusion
  924.5 1.3 fusion.7
  925.8 2.8 reshape.658
  (49 shorter events, 6.7 us)
Async XLA Ops:
  6.5 172.7 %all-reduce.19.cloned.1.call-start = ((), (), s32[]{:S(2)}) async-start(), calls=%async_computation.5 | async-start | bytes 2097152 | tf_op jit(solution)/shard_map/psum | solution.py:9
  14.5 281.3 %all-reduce.9.cloned.1.call-start = ((), (), s32[]{:S(2)}) async-start(), calls=%async_computation | async-start | bytes 1048576 | tf_op jit(solution)/shard_map/psum | solution.py:9
  179.2 3.4 copy-start.1
  179.2 3.4 copy-start.4
  182.5 1.4 copy-start.5
  185.0 275.2 %all-reduce.11.cloned.1.call-start = ((), (), s32[]{:S(2)}) async-start(), calls=%async_computation.1 | async-start | bytes 1048576 | tf_op jit(solution)/shard_map/psum | solution.py:9
  185.8 445.7 %all-reduce.17.cloned.1.call-start = ((), (), s32[]{:S(2)}) async-start(), calls=%async_computation.4 | async-start | bytes 2097152 | tf_op jit(solution)/shard_map/psum | solution.py:9
  460.3 3.6 copy-start
  460.3 6.5 copy-start.3
  473.4 280.7 %all-reduce.13.cloned.1.call-start = ((), (), s32[]{:S(2)}) async-start(), calls=%async_computation.2 | async-start | bytes 1048576 | tf_op jit(solution)/shard_map/psum | solution.py:9
  631.5 5.4 copy-start.2
  643.4 275.1 %all-reduce.15.cloned.1.call-start = ((), (), s32[]{:S(2)}) async-start(), calls=%async_computation.3 | async-start | bytes 1048576 | tf_op jit(solution)/shard_map/psum | solution.py:9
Sparse Core Ops, SparseCore 0:
  14.6 164.5 all-reduce.18
  185.2 110.5 all-reduce.8
  299.5 160.6 all-reduce.10
  473.6 157.9 all-reduce.16
  643.5 110.5 all-reduce.12
  757.7 160.6 all-reduce.14
where the time goes:
time: 936 us; the launch traced here: 935 us
  waiting for transfers between devices  872 us (93%)
  local copies, waits for them, and re-layouts  20.3 us (2%)
  other arithmetic  15.3 us (2%)
  matrix products  13.9 us (1%)
  between operations  13.7 us (1%)
    psum x6, waiting for transfers between devices, spread(): return lax.psum(block, axis)  871 us
  transfers between devices with their start and end apart: 6, of which 6 were waited for; matrix products, arithmetic and copies ran while one was open for 0% of the time, Pallas kernels for 0%

commit v1 on v0

--- a/solution.py
+++ b/solution.py
@@ -6,7 +6,7 @@
 
 def spread(block, axis, source):
     block = jnp.where(lax.axis_index(axis) == source, block, jnp.zeros_like(block))
-    return lax.psum(block, axis)
+    return jnp.sum(lax.all_gather(block, axis_name=axis), axis=0)
 
 
 def local(matrix, pivots, lower_inverse, upper_inverse):

time: 936 us -> 1120 us (1.20)
  the two profiles are of different devices: /device:TPU:64 before, /device:TPU:8 now
where the time goes in v1:
time: 1120 us
  waiting for transfers between devices  995 us (89%)
  other arithmetic  56.4 us (5%)
  local copies, waits for them, and re-layouts  40.8 us (4%)
  between operations  13.8 us (1%)
  matrix products  12.5 us (1%)
    all_gather x6, waiting for transfers between devices, spread(): return jnp.sum(lax.all_gather(block, axis_name=axis), axis=0)  701 us
    psum x2, waiting for transfers between devices, local(): incoming = lax.psum(picked, 'prow').astype(jnp.float32)  294 us
    reduce_sum x6, other arithmetic, spread(): return jnp.sum(lax.all_gather(block, axis_name=axis), axis=0)  44 us
    unnamed x19, local copies, waits for them, and re-layouts  22.6 us
  transfers between devices with their start and end apart: 8, of which 8 were waited for; matrix products, arithmetic and copies ran while one was open for 4% of the time, Pallas kernels for 0%

profile of v1, /device:TPU:8, one launch (start us, length us, event | category | flops | bytes accessed | tf_op | source)
XLA Modules:
  0.0 1119.4 jit_solution(15600051954794063893)
XLA Ops:
  13.4 146.0 %all-gather.12.cloned.1.call-done = bf16[32,256,1024]{2,1,0:T(8,128)(2,1)} async-done(((bf16[1,256,1024]{2,1,0:T(8,128)(2,1)}), bf16[32,256,1024]{2,1,0:T(8,128)(2,1)}) %all-gather.12.cloned.1.call-update) | async-done | bytes 16777232 | tf_op jit(solution)/shard_map/all_gather | solution.py:9
  159.4 9.1 reduce_sum.72
  168.5 2.8 scatter_fusion
  171.4 147.7 %all-reduce.3.cloned.1.call-done = bf16[256,1024]{1,0:T(8,128)(2,1)} async-done(((bf16[256,1024]{1,0:T(8,128)(2,1)}), bf16[256,1024]{1,0:T(8,128)(2,1)}) %all-reduce.3.cloned.1.call-update) | async-done | bytes 524304 | tf_op jit(solution)/shard_map/psum | solution.py:37
  323.0 56.4 %all-gather.14.cloned.1.call-done = bf16[16384,256]{1,0:T(8,128)(2,1)} async-done(((bf16[1024,256]{1,0:T(8,128)(2,1)}), bf16[16384,256]{1,0:T(8,128)(2,1)}) %all-gather.14.cloned.1.call-update) | async-done | bytes 8388624 | tf_op jit(solution)/shard_map/all_gather | solution.py:9
  379.4 4.8 reduce_sum.73
  384.2 152.2 %all-gather.16.cloned.1.call-done = bf16[8192,1024]{0,1:T(8,128)(2,1)} async-done(((bf16[256,1024]{0,1:T(8,128)(2,1)}), bf16[8192,1024]{0,1:T(8,128)(2,1)}) %all-gather.16.cloned.1.call-update) | async-done | bytes 16777232 | tf_op jit(solution)/shard_map/all_gather | solution.py:9
  536.4 10.3 copy.8
  546.7 8.1 bitcast_reduce_fusion.1
  555.8 2.3 and_select_fusion
  558.1 2.8 fusion.6
  563.5 3.4 gather_fusion.1
  567.9 137.0 %all-gather.18.cloned.1.call-done = bf16[8192,1024]{1,0:T(8,128)(2,1)} async-done(((bf16[256,1024]{1,0:T(8,128)(2,1)}), bf16[8192,1024]{1,0:T(8,128)(2,1)}) %all-gather.18.cloned.1.call-update) | async-done | bytes 16777232 | tf_op jit(solution)/shard_map/all_gather | solution.py:9
  705.0 9.1 reduce_sum.75
  714.0 4.8 scatter_fusion.1
  718.9 145.9 %all-reduce.5.cloned.1.call-done = bf16[256,1024]{1,0:T(8,128)(2,1)} async-done(((bf16[256,1024]{1,0:T(8,128)(2,1)}), bf16[256,1024]{1,0:T(8,128)(2,1)}) %all-reduce.5.cloned.1.call-update) | async-done | bytes 524304 | tf_op jit(solution)/shard_map/psum | solution.py:37
  864.8 2.3 fusion.5
  872.2 56.9 %all-gather.20.cloned.1.call-done = bf16[16384,256]{1,0:T(8,128)(2,1)} async-done(((bf16[1024,256]{1,0:T(8,128)(2,1)}), bf16[16384,256]{1,0:T(8,128)(2,1)}) %all-gather.20.cloned.1.call-update) | async-done | bytes 8388624 | tf_op jit(solution)/shard_map/all_gather | solution.py:9
  929.1 4.8 reduce_sum.76
  933.9 151.9 %all-gather.22.cloned.1.call-done = bf16[8192,1024]{0,1:T(8,128)(2,1)} async-done(((bf16[256,1024]{0,1:T(8,128)(2,1)}), bf16[8192,1024]{0,1:T(8,128)(2,1)}) %all-gather.22.cloned.1.call-update) | async-done | bytes 16777232 | tf_op jit(solution)/shard_map/all_gather | solution.py:9
  1085.8 10.3 copy.9
  1096.1 8.1 bitcast_reduce_fusion
  1105.2 3.4 and_select_fusion.1
  1109.8 2.8 reshape.668
  (67 shorter events, 22.3 us)
Async XLA Ops:
  6.5 152.9 %all-gather.12.cloned.1.call-start = ((), (), s32[]{:S(2)}) async-start(), calls=%async_computation | async-start | bytes 17301504 | tf_op jit(solution)/shard_map/all_gather | solution.py:9
  9.0 310.1 %all-reduce.3.cloned.1.call-start = ((), (), s32[]{:S(2)}) async-start(), calls=%async_computation.1 | async-start | bytes 1048576 | tf_op jit(solution)/shard_map/psum | solution.py:37
  9.0 2.1 copy-start.4
  13.3 366.1 %all-gather.14.cloned.1.call-start = ((), (), s32[]{:S(2)}) async-start(), calls=%async_computation.3 | async-start | bytes 8912896 | tf_op jit(solution)/shard_map/all_gather | solution.py:9
  168.5 150.5 %copy-start.5 = (bf16[2,256,256]{2,1,0:T(8,128)(2,1)S(1)}, bf16[2,256,256]{2,1,0:T(8,128)(2,1)}, u32[]{:S(2)}) copy-start(bf16[2,256,256]{2,1,0:T(8,128)(2,1)} %param.18) | copy-start | bytes 786436
  171.4 149.1 %copy-start.6 = (bf16[2,256,256]{2,1,0:T(8,128)(2,1)S(1)}, bf16[2,256,256]{2,1,0:T(8,128)(2,1)}, u32[]{:S(2)}) copy-start(bf16[2,256,256]{2,1,0:T(8,128)(2,1)} %param.19) | copy-start | bytes 786436
  319.1 1.2 copy-start.2
  321.6 214.8 %all-gather.16.cloned.1.call-start = ((), (), s32[]{:S(2)}) async-start(), calls=%async_computation.4 | async-start | bytes 17301504 | tf_op jit(solution)/shard_map/all_gather | solution.py:9
  322.2 382.7 %all-gather.18.cloned.1.call-start = ((), (), s32[]{:S(2)}) async-start(), calls=%async_computation.5 | async-start | bytes 17301504 | tf_op jit(solution)/shard_map/all_gather | solution.py:9
  555.8 5.1 copy-start
  563.2 301.6 %all-reduce.5.cloned.1.call-start = ((), (), s32[]{:S(2)}) async-start(), calls=%async_computation.2 | async-start | bytes 1048576 | tf_op jit(solution)/shard_map/psum | solution.py:37
  567.9 361.2 %all-gather.20.cloned.1.call-start = ((), (), s32[]{:S(2)}) async-start(), calls=%async_computation.6 | async-start | bytes 8912896 | tf_op jit(solution)/shard_map/all_gather | solution.py:9
  718.9 150.3 %copy-start.7 = (bf16[2,256,256]{2,1,0:T(8,128)(2,1)S(1)}, bf16[2,256,256]{2,1,0:T(8,128)(2,1)}, u32[]{:S(2)}) copy-start(bf16[2,256,256]{2,1,0:T(8,128)(2,1)} %param.19) | copy-start | bytes 786436
  864.8 2.3 copy-start.3
  871.3 214.5 %all-gather.22.cloned.1.call-start = ((), (), s32[]{:S(2)}) async-start(), calls=%async_computation.7 | async-start | bytes 17301504 | tf_op jit(solution)/shard_map/all_gather | solution.py:9
  1105.2 4.4 copy-start.1
Sparse Core Ops, SparseCore 0:
  10.5 148.8 all-gather.11
  162.8 156.1 all-reduce.2
  321.8 57.5 all-gather.13
  382.7 153.6 all-gather.15
  563.3 141.5 all-gather.17
  708.6 156.1 all-reduce.4
  871.5 57.5 all-gather.19
  932.1 153.6 all-gather.21
